TPU v7x, 128 devices: a whole 4x4x4 slice. The times are simulated.
128 devices in a mesh: chan: 16 (over z, y), seg: 4 (over x_hi, core), lag: 2 (over x_lo).
Axes of the slice: x: 4 (x_hi: 2, x_lo: 2; x = x_hi * 2 + x_lo), y: 4, z: 4, core: 2. Of those that a mesh axis runs over, the one named last changes fastest.
Arguments:
- spectra: bfloat16 [4, 10000, 2, 6144], P('seg', 'chan', None, 'lag'), may hold values from -6 to 6
- pair_local: int32 [16, 3, 256], replicated, may hold values from 0 to 624
- pair_partner: int32 [16, 3, 256], replicated, may hold values from 0 to 624, as said below
- pair_bin: int32 [16, 3, 256], replicated, may hold values from 0 to 1
- pair_owner: int32 [16, 3, 256], replicated, may hold values 0 or 1
- pair_count: int32 [16, 3], replicated, may hold values from 64 to 256, as said below
Outputs:
- stacks: float32 [10000, 2, 2048], P('chan', None, 'lag')
Inputs may be any that keep to these rules, and one draw needn't show every extreme that they name: `pair_partner`: in round 0 the two channels of a pair differ. `pair_count`: some block reaches 256 in some round.
All inputs are finite; a program needn't handle non-finite values.
Results may differ from a plain program's by a relative error of at most 0.0065.
Values may be sent and summed in bfloat16 or wider, within the bound.
No kernel may reach another device: no remote copies, remote signals or barrier semaphores. Data moves between devices by JAX's collectives and lax.ppermute only.
A program may use at most 128 MiB of HBM per device.

v0:
```python
import math
import jax
import jax.numpy as jnp
from jax import lax
from jax.sharding import PartitionSpec as P

FREQ = 6144
LAGS = 2048
ROUNDS = 3
BINS = 2


def shifted(block, axis, distance):
    devices = range(lax.axis_size(axis))
    route = [((i - distance) % len(devices), i) for i in devices]
    return lax.ppermute(block, axis, route)


def one_hot_rows(target_rows, mask_rows, total_rows):
    row_ids = jnp.arange(total_rows, dtype=jnp.int32)[:, None]
    return ((row_ids == target_rows[None, :]) & mask_rows[None, :]).astype(jnp.float32)


def bin_rows(selector, corr):
    return lax.dot_general(
        selector,
        corr,
        (((1,), (1,)), ((), ())),
        precision=lax.Precision.HIGHEST,
        preferred_element_type=jnp.float32,
    )


def per_device(spectra, pair_local, pair_partner, pair_bin, pair_owner, pair_count):
    block_index = lax.axis_index("chan")
    lag_index = lax.axis_index("lag")
    own_block = spectra[0]
    block_chans = own_block.shape[0]
    half_freq = own_block.shape[2]
    half_lags = LAGS // lax.axis_size("lag")
    total_rows = block_chans * BINS
    slot_count = pair_local.shape[2]
    freq_index = lag_index * half_freq + jnp.arange(half_freq, dtype=jnp.int32) + 1
    corr_scale = FREQ ** (-0.5)
    slot_ids = jnp.arange(slot_count, dtype=jnp.int32)
    local_stack = jnp.zeros((total_rows, half_lags), jnp.float32)
    for round_index in range(ROUNDS):
        first_index = pair_local[block_index, round_index]
        second_index = pair_partner[block_index, round_index]
        first = jnp.take(own_block, first_index, axis=0).astype(jnp.float32)
        if round_index == 0:
            second = jnp.take(own_block, second_index, axis=0).astype(jnp.float32)
        else:
            partner_block = shifted(own_block, "chan", -round_index)
            second = jnp.take(partner_block, second_index, axis=0).astype(jnp.float32)
        cross_real = first[:, 0] * second[:, 0] + first[:, 1] * second[:, 1]
        cross_imag = first[:, 1] * second[:, 0] - first[:, 0] * second[:, 1]
        cross = jnp.concatenate([cross_real, cross_imag], axis=1).astype(jnp.bfloat16)
        block_rows = math.gcd(lax.axis_size("lag") * half_lags, 512)

        def one_block(offset):
            taus = offset + jnp.arange(block_rows, dtype=jnp.int32) - LAGS // 2
            phase = jnp.mod(taus[:, None] * freq_index[None, :], 2 * FREQ)
            angle = phase.astype(jnp.float32) * (math.pi / FREQ)
            table = jnp.concatenate([jnp.cos(angle), -jnp.sin(angle)], axis=1).astype(jnp.bfloat16)
            return (
                lax.dot_general(
                    table, cross, (((1,), (1,)), ((), ())), preferred_element_type=jnp.float32
                )
                * corr_scale
            )

        offsets = (
            jnp.arange(lax.axis_size("lag") * half_lags // block_rows, dtype=jnp.int32) * block_rows
        )
        corr = lax.psum_scatter(
            lax.map(one_block, offsets).reshape(lax.axis_size("lag") * half_lags, slot_count),
            "lag",
            scatter_dimension=0,
            tiled=True,
        )
        live = slot_ids < pair_count[block_index, round_index]
        owners = pair_owner[block_index, round_index]
        bins_now = pair_bin[block_index, round_index]
        own_rows = jnp.where(owners == 0, first_index, second_index) * BINS + bins_now
        if round_index == 0:
            local_stack = bin_rows(one_hot_rows(own_rows, live, total_rows), corr)
        else:
            mine_rows = first_index * BINS + bins_now
            local_stack = local_stack + bin_rows(
                one_hot_rows(mine_rows, live & (owners == 0), total_rows), corr
            )
            partner_rows = second_index * BINS + bins_now
            partner_stack = bin_rows(
                one_hot_rows(partner_rows, live & (owners == 1), total_rows), corr
            )
            local_stack = local_stack + shifted(partner_stack, "chan", round_index)
    local_stack = lax.psum(local_stack, "seg")
    return local_stack.reshape(block_chans, BINS, half_lags)


def solution(mesh):
    return jax.shard_map(
        per_device,
        mesh=mesh,
        in_specs=(P("seg", "chan", None, "lag"), P(), P(), P(), P(), P()),
        out_specs=P("chan", None, "lag"),
        check_vma=False,
    )
```

profile of v0, /device:TPU:1, one launch (start us, length us, event | category | flops | bytes accessed | tf_op | source)
XLA Modules:
  0.0 1053.6 jit_solution(12858665571062625390)
XLA Ops:
  6.5 7.0 collective-permute-start
  16.7 16.3 %gather_fusion.2 = bf16[256,2,3072]{2,1,0:T(2,128)(2,1)S(1)} fusion(bf16[625,2,3072]{2,1,0:T(2,128)(2,1)} %bitcast.81, s32[1024]{0:T(1024)S(1)} %pad_clamp_fusion.3), kind=kCustom, calls=%fused_computation.2.clone | custom fusion | bytes 6292480 | tf_op jit(solution)/shard_map/jit(_take)/gather | solution.py:50
  35.0 16.2 %gather_fusion = bf16[256,2,3072]{2,1,0:T(2,128)(2,1)} fusion(bf16[625,2,3072]{2,1,0:T(2,128)(2,1)} %bitcast.82, s32[1024]{0:T(1024)S(1)} %get-tuple-element.328), kind=kCustom, calls=%fused_computation.clone | custom fusion | bytes 6292480 | tf_op jit(solution)/shard_map/jit(_take)/gather | solution.py:50
  51.2 16.5 %gather_fusion.1 = bf16[256,2,3072]{2,1,0:T(2,128)(2,1)} fusion(bf16[625,2,3072]{2,1,0:T(2,128)(2,1)} %bitcast.83, s32[1024]{0:T(1024)S(1)} %get-tuple-element.327), kind=kCustom, calls=%fused_computation.1.clone | custom fusion | bytes 6292480 | tf_op jit(solution)/shard_map/jit(_take)/gather | solution.py:52
  68.2 16.6 %gather_fusion.4 = bf16[256,2,3072]{2,1,0:T(2,128)(2,1)} fusion(bf16[625,2,3072]{2,1,0:T(2,128)(2,1)} %bitcast.84, s32[1024]{0:T(1024)S(1)} %pad_clamp_fusion.1), kind=kCustom, calls=%fused_computation.4.clone | custom fusion | bytes 6292480 | tf_op jit(solution)/shard_map/jit(_take)/gather | solution.py:50
  85.0 5.5 fusion.65
  90.5 5.5 fusion.63
  96.0 5.6 fusion.67
  101.6 240.8 %collective-permute-done = bf16[625,2,3072]{2,1,0:T(2,128)(2,1)} collective-permute-done((bf16[625,2,3072]{2,1,0:T(2,128)(2,1)}, bf16[625,2,3072]{2,1,0:T(2,128)(2,1)}, u32[]{:S(2)}, u32[]{:S(2)}) %collective-permute-start) | collective-permute-done | bytes 7680032 | tf_op jit(solution)/shard_map/ppermute | solution.py:16
  342.4 16.5 %gather_fusion.3 = bf16[256,2,3072]{2,1,0:T(2,128)(2,1)} fusion(bf16[625,2,3072]{2,1,0:T(2,128)(2,1)} %collective-permute-done, s32[1024]{0:T(1024)S(1)} %pad_clamp_fusion.2), kind=kCustom, calls=%fused_computation.3.clone | custom fusion | bytes 6292480 | tf_op jit(solution)/shard_map/jit(_take)/gather | solution.py:55
  358.9 7.6 fusion.66
  366.6 12.3 %add_convert_fusion.1 = (bf16[256,1,3072]{2,1,0:T(2,128)(2,1)S(1)}, bf16[256,1,3072]{2,1,0:T(2,128)(2,1)S(1)}) fusion(f32[256,2,3072]{2,1,0:T(2,128)} %fusion.66, f32[256,2,3072]{2,1,0:T(2,128)S(1)} %bitcast.78), kind=kLoop, calls=%fused_computation.85 | loop fusion | flops 6291456 | bytes 15728640 | tf_op jit(solution)/shard_map/convert.13
  381.9 118.2 %while.40 = (s32[]{:T(128)}, f32[4,512,256]{2,1,0:T(8,128)S(1)}, s32[4]{0:T(128)S(1)}, bf16[256,6144]{1,0:T(8,128)(2,1)}, s32[]{:T(128)}, /*index=5*/s32[]{:T(128)}) while((s32[]{:T(128)}, f32[4,512,256]{2,1,0:T(8,128)S(1)}, s32[4]{0:T(128)S(1)}, bf16[256,6144]{1,0:T(8,128)(2,1)}, s32[]{:T(128)}, /*index=5*/s32[]{:T(128)}) %tuple.118), condition=%wide.region_4.6_spmd.clone, body=%wide.region_3.5_spmd.clone.sunk | while | flops 1642208256 | bytes 28864632 | solution.py:77
  383.3 26.3 %cosine_convert_fusion.7 = (bf16[512,3072]{1,0:T(8,128)(2,1)S(1)}, bf16[512,3072]{1,0:T(8,128)(2,1)S(1)}) fusion(s32[3072]{0:T(1024)S(1)} %add_add_fusion.15, s32[512]{0:T(512)S(1)} %add_add_fusion.16), kind=kLoop, calls=%fused_computation.36.clone.1 | loop fusion | flops 18874368 | bytes 6305792 | tf_op jit(solution)/shard_map/convert.2
  412.8 26.3 %cosine_convert_fusion.7 = (bf16[512,3072]{1,0:T(8,128)(2,1)S(1)}, bf16[512,3072]{1,0:T(8,128)(2,1)S(1)}) fusion(s32[3072]{0:T(1024)S(1)} %add_add_fusion.15, s32[512]{0:T(512)S(1)} %add_add_fusion.16), kind=kLoop, calls=%fused_computation.36.clone.1 | loop fusion | flops 18874368 | bytes 6305792 | tf_op jit(solution)/shard_map/convert.2
  442.4 26.3 %cosine_convert_fusion.7 = (bf16[512,3072]{1,0:T(8,128)(2,1)S(1)}, bf16[512,3072]{1,0:T(8,128)(2,1)S(1)}) fusion(s32[3072]{0:T(1024)S(1)} %add_add_fusion.15, s32[512]{0:T(512)S(1)} %add_add_fusion.16), kind=kLoop, calls=%fused_computation.36.clone.1 | loop fusion | flops 18874368 | bytes 6305792 | tf_op jit(solution)/shard_map/convert.2
  471.9 26.3 %cosine_convert_fusion.7 = (bf16[512,3072]{1,0:T(8,128)(2,1)S(1)}, bf16[512,3072]{1,0:T(8,128)(2,1)S(1)}) fusion(s32[3072]{0:T(1024)S(1)} %add_add_fusion.15, s32[512]{0:T(512)S(1)} %add_add_fusion.16), kind=kLoop, calls=%fused_computation.36.clone.1 | loop fusion | flops 18874368 | bytes 6305792 | tf_op jit(solution)/shard_map/convert.2
  501.7 16.7 %gather_fusion.5 = bf16[256,2,3072]{2,1,0:T(2,128)(2,1)} fusion(bf16[625,2,3072]{2,1,0:T(2,128)(2,1)} %collective-permute-done.2, s32[1024]{0:T(1024)S(1)} %pad_clamp_fusion), kind=kCustom, calls=%fused_computation.5.clone | custom fusion | bytes 6292480 | tf_op jit(solution)/shard_map/jit(_take)/gather | solution.py:55
  518.4 7.6 fusion.68
  526.0 12.4 %add_convert_fusion = (bf16[256,1,3072]{2,1,0:T(2,128)(2,1)S(1)}, bf16[256,1,3072]{2,1,0:T(2,128)(2,1)S(1)}) fusion(f32[256,2,3072]{2,1,0:T(2,128)} %fusion.68, f32[256,2,3072]{2,1,0:T(2,128)S(1)} %bitcast.76), kind=kLoop, calls=%fused_computation.83 | loop fusion | flops 6291456 | bytes 15728640 | tf_op jit(solution)/shard_map/convert.9
  542.8 121.2 %while.41 = (s32[]{:T(128)}, f32[4,512,256]{2,1,0:T(8,128)}, s32[4]{0:T(128)S(1)}, bf16[256,6144]{1,0:T(8,128)(2,1)}, s32[]{:T(128)}, /*index=5*/s32[]{:T(128)}) while((s32[]{:T(128)}, f32[4,512,256]{2,1,0:T(8,128)}, s32[4]{0:T(128)S(1)}, bf16[256,6144]{1,0:T(8,128)(2,1)}, s32[]{:T(128)}, /*index=5*/s32[]{:T(128)}) %tuple.132), condition=%wide.region_7.9_spmd.clone, body=%wide.region_6.8_spmd.clone.sunk | while | flops 1642208256 | bytes 28865140 | solution.py:77
  544.4 26.3 %cosine_convert_fusion.8 = (bf16[512,3072]{1,0:T(8,128)(2,1)S(1)}, bf16[512,3072]{1,0:T(8,128)(2,1)S(1)}) fusion(s32[3072]{0:T(1024)S(1)} %add_add_fusion.17, s32[512]{0:T(512)S(1)} %add_add_fusion.18), kind=kLoop, calls=%fused_computation.55.clone.1 | loop fusion | flops 18874368 | bytes 6305792 | tf_op jit(solution)/shard_map/convert.4
  570.7 2.6 fusion.122
  574.6 26.3 %cosine_convert_fusion.8 = (bf16[512,3072]{1,0:T(8,128)(2,1)S(1)}, bf16[512,3072]{1,0:T(8,128)(2,1)S(1)}) fusion(s32[3072]{0:T(1024)S(1)} %add_add_fusion.17, s32[512]{0:T(512)S(1)} %add_add_fusion.18), kind=kLoop, calls=%fused_computation.55.clone.1 | loop fusion | flops 18874368 | bytes 6305792 | tf_op jit(solution)/shard_map/convert.4
  601.0 2.6 fusion.122
  604.8 26.3 %cosine_convert_fusion.8 = (bf16[512,3072]{1,0:T(8,128)(2,1)S(1)}, bf16[512,3072]{1,0:T(8,128)(2,1)S(1)}) fusion(s32[3072]{0:T(1024)S(1)} %add_add_fusion.17, s32[512]{0:T(512)S(1)} %add_add_fusion.18), kind=kLoop, calls=%fused_computation.55.clone.1 | loop fusion | flops 18874368 | bytes 6305792 | tf_op jit(solution)/shard_map/convert.4
  631.2 2.6 fusion.122
  635.0 26.3 %cosine_convert_fusion.8 = (bf16[512,3072]{1,0:T(8,128)(2,1)S(1)}, bf16[512,3072]{1,0:T(8,128)(2,1)S(1)}) fusion(s32[3072]{0:T(1024)S(1)} %add_add_fusion.17, s32[512]{0:T(512)S(1)} %add_add_fusion.18), kind=kLoop, calls=%fused_computation.55.clone.1 | loop fusion | flops 18874368 | bytes 6305792 | tf_op jit(solution)/shard_map/convert.4
  661.4 2.6 fusion.122
  664.1 2.8 fusion.64
  667.0 12.0 %add_convert_fusion.2 = (bf16[256,1,3072]{2,1,0:T(2,128)(2,1)S(1)}, bf16[256,1,3072]{2,1,0:T(2,128)(2,1)S(1)}) fusion(f32[256,2,3072]{2,1,0:T(2,128)S(1)} %fusion.64, f32[256,2,3072]{2,1,0:T(2,128)} %fusion.63), kind=kLoop, calls=%fused_computation.87 | loop fusion | flops 6291456 | bytes 15728640 | tf_op jit(solution)/shard_map/convert.17
  684.0 5.8 fusion.75
  689.8 11.1 %reduce-scatter.8.cloned.1.call-done = f32[1024,256]{1,0:T(8,128)} async-done(((f32[2048,256]{1,0:T(8,128)}), f32[1024,256]{1,0:T(8,128)}) %reduce-scatter.8.cloned.1.call-update) | async-done | bytes 1048592 | tf_op jit(solution)/shard_map/reduce_scatter | solution.py:76
  701.0 5.7 fusion.81
  706.7 2.7 collective-permute-start.3
  709.6 117.7 %while.39 = (s32[]{:T(128)}, f32[4,512,256]{2,1,0:T(8,128)S(1)}, s32[4]{0:T(128)S(1)}, bf16[256,6144]{1,0:T(8,128)(2,1)}, s32[]{:T(128)}, /*index=5*/s32[]{:T(128)}) while((s32[]{:T(128)}, f32[4,512,256]{2,1,0:T(8,128)S(1)}, s32[4]{0:T(128)S(1)}, bf16[256,6144]{1,0:T(8,128)(2,1)}, s32[]{:T(128)}, /*index=5*/s32[]{:T(128)}) %tuple.133), condition=%wide.region_1.3_spmd.clone, body=%wide.region_0.0_spmd.clone.sunk | while | flops 1642208256 | bytes 28864632 | solution.py:77
  710.9 26.3 %cosine_convert_fusion.6 = (bf16[512,3072]{1,0:T(8,128)(2,1)S(1)}, bf16[512,3072]{1,0:T(8,128)(2,1)S(1)}) fusion(s32[3072]{0:T(1024)S(1)} %add_add_fusion.13, s32[512]{0:T(512)S(1)} %add_add_fusion.14), kind=kLoop, calls=%fused_computation.17.clone.1 | loop fusion | flops 18874368 | bytes 6305792 | tf_op jit(solution)/shard_map/convert
  740.3 26.3 %cosine_convert_fusion.6 = (bf16[512,3072]{1,0:T(8,128)(2,1)S(1)}, bf16[512,3072]{1,0:T(8,128)(2,1)S(1)}) fusion(s32[3072]{0:T(1024)S(1)} %add_add_fusion.13, s32[512]{0:T(512)S(1)} %add_add_fusion.14), kind=kLoop, calls=%fused_computation.17.clone.1 | loop fusion | flops 18874368 | bytes 6305792 | tf_op jit(solution)/shard_map/convert
  769.7 26.3 %cosine_convert_fusion.6 = (bf16[512,3072]{1,0:T(8,128)(2,1)S(1)}, bf16[512,3072]{1,0:T(8,128)(2,1)S(1)}) fusion(s32[3072]{0:T(1024)S(1)} %add_add_fusion.13, s32[512]{0:T(512)S(1)} %add_add_fusion.14), kind=kLoop, calls=%fused_computation.17.clone.1 | loop fusion | flops 18874368 | bytes 6305792 | tf_op jit(solution)/shard_map/convert
  799.2 26.3 %cosine_convert_fusion.6 = (bf16[512,3072]{1,0:T(8,128)(2,1)S(1)}, bf16[512,3072]{1,0:T(8,128)(2,1)S(1)}) fusion(s32[3072]{0:T(1024)S(1)} %add_add_fusion.13, s32[512]{0:T(512)S(1)} %add_add_fusion.14), kind=kLoop, calls=%fused_computation.17.clone.1 | loop fusion | flops 18874368 | bytes 6305792 | tf_op jit(solution)/shard_map/convert
  830.8 32.4 %reduce-scatter.4.cloned.1.call-done = f32[1024,256]{1,0:T(8,128)} async-done(((f32[2048,256]{1,0:T(8,128)}), f32[1024,256]{1,0:T(8,128)}) %reduce-scatter.4.cloned.1.call-update) | async-done | bytes 1048592 | tf_op jit(solution)/shard_map/reduce_scatter | solution.py:76
  863.3 3.6 fusion.70
  866.9 2.3 fusion.78
  869.1 47.5 %collective-permute-done.3 = f32[1250,1024]{1,0:T(8,128)} collective-permute-done((f32[1250,1024]{1,0:T(8,128)}, f32[1250,1024]{1,0:T(8,128)}, u32[]{:S(2)}, u32[]{:S(2)}) %collective-permute-start.3) | collective-permute-done | bytes 5120032 | tf_op jit(solution)/shard_map/ppermute | solution.py:16
  916.6 9.4 add_add_fusion.6
  926.0 7.3 reshape.172
  933.3 106.7 %all-reduce.2.cloned.1.call-done = f32[625,2,1024]{2,1,0:T(2,128)} async-done(((f32[625,2,1024]{2,1,0:T(2,128)}), f32[625,2,1024]{2,1,0:T(2,128)}) %all-reduce.2.cloned.1.call-update) | async-done | bytes 5120016 | tf_op jit(solution)/shard_map/psum | solution.py:98
  1040.1 6.5 copy.63
  (150 shorter events, 53.3 us)
Async XLA Ops:
  6.5 677.5 %reduce-scatter.6.cloned.1.call-start = ((), (), s32[]{:S(2)}) async-start(), calls=%async_computation.4 | async-start | bytes 3145728 | tf_op jit(solution)/shard_map/reduce_scatter | solution.py:76
  6.5 335.9 %collective-permute-start = (bf16[625,2,3072]{2,1,0:T(2,128)(2,1)}, bf16[625,2,3072]{2,1,0:T(2,128)(2,1)}, u32[]{:S(2)}, u32[]{:S(2)}) collective-permute-start(bf16[625,2,3072]{2,1,0:T(2,128)(2,1)} %bitcast.79), channel_id=1, source_target_pairs={{8,0},{16,8},{24,16},{32,24},{40,32},{48,40},{56,48},{64,56},{72,6... | collective-permute-start | bytes 23040008 | tf_op jit(solution)/shard_map/ppermute | solution.py:16
  13.6 488.1 %collective-permute-start.2 = (bf16[625,2,3072]{2,1,0:T(2,128)(2,1)}, bf16[625,2,3072]{2,1,0:T(2,128)(2,1)}, u32[]{:S(2)}, u32[]{:S(2)}) collective-permute-start(bf16[625,2,3072]{2,1,0:T(2,128)(2,1)} %bitcast.80), channel_id=1, source_target_pairs={{16,0},{24,8},{32,16},{40,24},{48,32},{56,40},{64,48},{72,56},{80,... | collective-permute-start | bytes 23040008 | tf_op jit(solution)/shard_map/ppermute | solution.py:16
  85.0 5.5 copy-start.1
  90.5 5.5 copy-start.2
  342.4 24.1 %slice-start.2 = ((s8[6291456]{0:T(1024)(128)(4,1)}), s8[2097152]{0:T(1024)(128)(4,1)S(1)}, s32[]{:S(2)}) async-start(s8[6291456]{0:T(1024)(128)(4,1)} %bitcast.77), calls=%async_computation.9 | async-start | bytes 4194304
  358.9 7.6 slice-start.3
  383.3 26.3 %copy-start.8 = (bf16[256,6144]{1,0:T(8,128)(2,1)S(1)}, bf16[256,6144]{1,0:T(8,128)(2,1)}, u32[]{:S(2)}) copy-start(bf16[256,6144]{1,0:T(8,128)(2,1)} %get-tuple-element.467) | copy-start | bytes 9437188 | tf_op jit(solution)/shard_map/while
  412.8 26.3 %copy-start.8 = (bf16[256,6144]{1,0:T(8,128)(2,1)S(1)}, bf16[256,6144]{1,0:T(8,128)(2,1)}, u32[]{:S(2)}) copy-start(bf16[256,6144]{1,0:T(8,128)(2,1)} %get-tuple-element.467) | copy-start | bytes 9437188 | tf_op jit(solution)/shard_map/while
  442.4 26.3 %copy-start.8 = (bf16[256,6144]{1,0:T(8,128)(2,1)S(1)}, bf16[256,6144]{1,0:T(8,128)(2,1)}, u32[]{:S(2)}) copy-start(bf16[256,6144]{1,0:T(8,128)(2,1)} %get-tuple-element.467) | copy-start | bytes 9437188 | tf_op jit(solution)/shard_map/while
  471.9 26.3 %copy-start.8 = (bf16[256,6144]{1,0:T(8,128)(2,1)S(1)}, bf16[256,6144]{1,0:T(8,128)(2,1)}, u32[]{:S(2)}) copy-start(bf16[256,6144]{1,0:T(8,128)(2,1)} %get-tuple-element.467) | copy-start | bytes 9437188 | tf_op jit(solution)/shard_map/while
  500.1 1.4 copy-start.4
  501.6 199.4 %reduce-scatter.8.cloned.1.call-start = ((), (), s32[]{:S(2)}) async-start(), calls=%async_computation.5 | async-start | bytes 3145728 | tf_op jit(solution)/shard_map/reduce_scatter | solution.py:76
  501.7 24.3 %slice-start = ((s8[6291456]{0:T(1024)(128)(4,1)}), s8[2097152]{0:T(1024)(128)(4,1)S(1)}, s32[]{:S(2)}) async-start(s8[6291456]{0:T(1024)(128)(4,1)} %bitcast.75), calls=%async_computation.7 | async-start | bytes 4194304
  518.4 7.6 slice-start.1
  542.8 121.3 %copy-start = (bf16[256,2,3072]{2,1,0:T(2,128)(2,1)S(1)}, bf16[256,2,3072]{2,1,0:T(2,128)(2,1)}, u32[]{:S(2)}) copy-start(bf16[256,2,3072]{2,1,0:T(2,128)(2,1)} %gather_fusion.1) | copy-start | bytes 9437188
  544.4 26.3 %copy-start.9 = (bf16[256,6144]{1,0:T(8,128)(2,1)S(1)}, bf16[256,6144]{1,0:T(8,128)(2,1)}, u32[]{:S(2)}) copy-start(bf16[256,6144]{1,0:T(8,128)(2,1)} %get-tuple-element.449) | copy-start | bytes 9437188 | tf_op jit(solution)/shard_map/while
  574.6 26.3 %copy-start.9 = (bf16[256,6144]{1,0:T(8,128)(2,1)S(1)}, bf16[256,6144]{1,0:T(8,128)(2,1)}, u32[]{:S(2)}) copy-start(bf16[256,6144]{1,0:T(8,128)(2,1)} %get-tuple-element.449) | copy-start | bytes 9437188 | tf_op jit(solution)/shard_map/while
  604.8 26.3 %copy-start.9 = (bf16[256,6144]{1,0:T(8,128)(2,1)S(1)}, bf16[256,6144]{1,0:T(8,128)(2,1)}, u32[]{:S(2)}) copy-start(bf16[256,6144]{1,0:T(8,128)(2,1)} %get-tuple-element.449) | copy-start | bytes 9437188 | tf_op jit(solution)/shard_map/while
  635.0 26.3 %copy-start.9 = (bf16[256,6144]{1,0:T(8,128)(2,1)S(1)}, bf16[256,6144]{1,0:T(8,128)(2,1)}, u32[]{:S(2)}) copy-start(bf16[256,6144]{1,0:T(8,128)(2,1)} %get-tuple-element.449) | copy-start | bytes 9437188 | tf_op jit(solution)/shard_map/while
  664.0 199.2 %reduce-scatter.4.cloned.1.call-start = ((), (), s32[]{:S(2)}) async-start(), calls=%async_computation.3 | async-start | bytes 3145728 | tf_op jit(solution)/shard_map/reduce_scatter | solution.py:76
  679.5 0.7 copy-start.15
  689.8 179.3 %collective-permute-start.1 = (f32[1250,1024]{1,0:T(8,128)}, f32[1250,1024]{1,0:T(8,128)}, u32[]{:S(2)}, u32[]{:S(2)}) collective-permute-start(f32[1250,1024]{1,0:T(8,128)} %fusion.75), channel_id=1, source_target_pairs={{120,0},{0,8},{8,16},{16,24},{24,32},{32,40},{40,48},{48,56},{56,6... | collective-permute-start | bytes 15360008 | tf_op jit(solution)/shard_map/ppermute | solution.py:16
  706.7 209.9 %collective-permute-start.3 = (f32[1250,1024]{1,0:T(8,128)}, f32[1250,1024]{1,0:T(8,128)}, u32[]{:S(2)}, u32[]{:S(2)}) collective-permute-start(f32[1250,1024]{1,0:T(8,128)} %fusion.81), channel_id=1, source_target_pairs={{112,0},{120,8},{0,16},{8,24},{16,32},{24,40},{32,48},{40,56},{48,... | collective-permute-start | bytes 15360008 | tf_op jit(solution)/shard_map/ppermute | solution.py:16
  709.6 120.0 %copy-start.13 = (pred[256]{0:T(512)(128)(4,1)S(1)}, pred[256]{0:T(512)(128)(4,1)}, u32[]{:S(2)}) copy-start(pred[256]{0:T(512)(128)(4,1)} %get-tuple-element.249) | copy-start | bytes 772
  709.6 120.0 %copy-start.14 = (pred[256]{0:T(512)(128)(4,1)S(1)}, pred[256]{0:T(512)(128)(4,1)}, u32[]{:S(2)}) copy-start(pred[256]{0:T(512)(128)(4,1)} %get-tuple-element.253) | copy-start | bytes 772
  709.6 153.6 %copy-start.11 = (s32[256]{0:T(256)S(1)}, s32[256]{0:T(256)}, u32[]{:S(2)}) copy-start(s32[256]{0:T(256)} %get-tuple-element.312) | copy-start | bytes 3076
  710.9 26.3 %copy-start.7 = (bf16[256,6144]{1,0:T(8,128)(2,1)S(1)}, bf16[256,6144]{1,0:T(8,128)(2,1)}, u32[]{:S(2)}) copy-start(bf16[256,6144]{1,0:T(8,128)(2,1)} %get-tuple-element.485) | copy-start | bytes 9437188 | tf_op jit(solution)/shard_map/while
  740.3 26.3 %copy-start.7 = (bf16[256,6144]{1,0:T(8,128)(2,1)S(1)}, bf16[256,6144]{1,0:T(8,128)(2,1)}, u32[]{:S(2)}) copy-start(bf16[256,6144]{1,0:T(8,128)(2,1)} %get-tuple-element.485) | copy-start | bytes 9437188 | tf_op jit(solution)/shard_map/while
  769.7 26.3 %copy-start.7 = (bf16[256,6144]{1,0:T(8,128)(2,1)S(1)}, bf16[256,6144]{1,0:T(8,128)(2,1)}, u32[]{:S(2)}) copy-start(bf16[256,6144]{1,0:T(8,128)(2,1)} %get-tuple-element.485) | copy-start | bytes 9437188 | tf_op jit(solution)/shard_map/while
  799.2 26.3 %copy-start.7 = (bf16[256,6144]{1,0:T(8,128)(2,1)S(1)}, bf16[256,6144]{1,0:T(8,128)(2,1)}, u32[]{:S(2)}) copy-start(bf16[256,6144]{1,0:T(8,128)(2,1)} %get-tuple-element.485) | copy-start | bytes 9437188 | tf_op jit(solution)/shard_map/while
  827.4 1.3 copy-start.3
  828.7 211.4 %all-reduce.2.cloned.1.call-start = ((), (), s32[]{:S(2)}) async-start(), calls=%async_computation.6 | async-start | bytes 10240000 | tf_op jit(solution)/shard_map/psum | solution.py:98
  863.3 3.6 copy-start.6
  863.3 3.6 copy-start.10
  866.8 49.8 %copy-start.5 = (f32[1024,256]{1,0:T(8,128)S(1)}, f32[1024,256]{1,0:T(8,128)}, u32[]{:S(2)}) copy-start(f32[1024,256]{1,0:T(8,128)} %reduce-scatter.6.cloned.1.call-done) | copy-start | bytes 3145732
  866.9 49.7 %copy-start.12 = (s32[256]{0:T(256)S(1)}, s32[256]{0:T(256)}, u32[]{:S(2)}) copy-start(s32[256]{0:T(256)} %get-tuple-element.308) | copy-start | bytes 3076
Sparse Core Ops, SparseCore 0:
  501.7 36.7 reduce-scatter.5
  664.2 36.7 reduce-scatter.7
  828.8 34.3 reduce-scatter.3
  933.5 106.5 all-reduce.1
where the time goes:
time: 1060 us; the launch traced here: 1050 us
  waiting for transfers between devices  439 us (41%)
  other arithmetic  407 us (38%)
  local copies, waits for them, and re-layouts  131 us (12%)
  matrix products  51.9 us (5%)
  between operations  13.9 us (1%)
    another operation x15, other arithmetic  353 us
    ppermute x4, waiting for transfers between devices, shifted(): return lax.ppermute(block, axis, route)  288 us
    psum x1, waiting for transfers between devices, per_device(): local_stack = lax.psum(local_stack, 'seg')  107 us
    gather x3, local copies, waits for them, and re-layouts, per_device(): first = jnp.take(own_block, first_index, axis=0).astype(jnp.float32)  49.2 us
    reduce_scatter x3, waiting for transfers between devices, per_device(): lax.psum_scatter(lax.map(one_block, offsets).reshape(lax.axis_size('lag')...  43.5 us
    gather x2, local copies, waits for them, and re-layouts, per_device(): second = jnp.take(partner_block, second_index, axis=0).astype(jnp.float32)  33.3 us
    dot_general x5, matrix products, bin_rows(): lax.dot_general(selector, corr, (((1,), (1,)), ((), ())), precision=lax.P...  26.8 us
    dot_general x12, matrix products, one_block(): lax.dot_general(table, cross, (((1,), (1,)), ((), ())), preferred_element...  25.1 us
  transfers between devices with their start and end apart: 8, of which 5 were waited for; matrix products, arithmetic and copies ran while one was open for 53% of the time, Pallas kernels for 0%

commit v1 on v0

--- a/solution.py
+++ b/solution.py
@@ -1,13 +1,22 @@
+import functools
 import math
 import jax
 import jax.numpy as jnp
 from jax import lax
 from jax.sharding import PartitionSpec as P
+from jax.lax import all_gather
 
 FREQ = 6144
 LAGS = 2048
 ROUNDS = 3
 BINS = 2
+
+
+def obtain_stocks(x_local, shard_axis):
+    return all_gather(x_local, shard_axis).sum(axis=0)
+
+
+quarters_choose = functools.partial(obtain_stocks, shard_axis="seg")
 
 
 def shifted(block, axis, distance):
@@ -95,7 +104,7 @@
                 one_hot_rows(partner_rows, live & (owners == 1), total_rows), corr
             )
             local_stack = local_stack + shifted(partner_stack, "chan", round_index)
-    local_stack = lax.psum(local_stack, "seg")
+    local_stack = quarters_choose(local_stack)
     return local_stack.reshape(block_chans, BINS, half_lags)
 
 

time: 1060 us -> 1090 us (1.028)
  waiting for transfers between devices: 439 us -> 464 us
    all_gather x0 -> x1, waiting for transfers between devices: none -> 132 us  [obtain_stocks(): return all_gather(x_local, shard_axis).sum(axis=0)]
    psum x1 -> x0, waiting for transfers between devices: 107 us -> none  [per_device(): local_stack = lax.psum(local_stack, 'seg')]
  transfers between devices with their start and end apart: 8 -> 8, of which waited for: 5 -> 5; matrix products, arithmetic and copies ran while one was open for 53% -> 52% of each run, Pallas kernels for 0% -> 0%
where the time goes in v1:
time: 1090 us; the launch traced here: 1080 us
  waiting for transfers between devices  464 us (43%)
  other arithmetic  417 us (38%)
  local copies, waits for them, and re-layouts  124 us (11%)
  matrix products  51.9 us (5%)
  between operations  13.9 us (1%)
    another operation x15, other arithmetic  353 us
    ppermute x4, waiting for transfers between devices, shifted(): return lax.ppermute(block, axis, route)  288 us
    all_gather x1, waiting for transfers between devices, obtain_stocks(): return all_gather(x_local, shard_axis).sum(axis=0)  132 us
    gather x3, local copies, waits for them, and re-layouts, per_device(): first = jnp.take(own_block, first_index, axis=0).astype(jnp.float32)  49.2 us
    reduce_scatter x3, waiting for transfers between devices, per_device(): lax.psum_scatter(lax.map(one_block, offsets).reshape(lax.axis_size('lag')...  43.5 us
    gather x2, local copies, waits for them, and re-layouts, per_device(): second = jnp.take(partner_block, second_index, axis=0).astype(jnp.float32)  33.3 us
    dot_general x5, matrix products, bin_rows(): lax.dot_general(selector, corr, (((1,), (1,)), ((), ())), precision=lax.P...  26.7 us
    dot_general x12, matrix products, one_block(): lax.dot_general(table, cross, (((1,), (1,)), ((), ())), preferred_element...  25.1 us
  transfers between devices with their start and end apart: 8, of which 5 were waited for; matrix products, arithmetic and copies ran while one was open for 52% of the time, Pallas kernels for 0%

profile of v1, /device:TPU:1, one launch (start us, length us, event | category | flops | bytes accessed | tf_op | source)
XLA Modules:
  0.0 1082.7 jit_solution(11990625993006909180)
XLA Ops:
  6.5 7.0 collective-permute-start
  16.7 16.3 %gather_fusion.2 = bf16[256,2,3072]{2,1,0:T(2,128)(2,1)S(1)} fusion(bf16[625,2,3072]{2,1,0:T(2,128)(2,1)} %bitcast.83, s32[1024]{0:T(1024)S(1)} %pad_clamp_fusion.3), kind=kCustom, calls=%fused_computation.2.clone | custom fusion | bytes 6292480 | tf_op jit(solution)/shard_map/jit(_take)/gather | solution.py:59
  35.0 16.2 %gather_fusion = bf16[256,2,3072]{2,1,0:T(2,128)(2,1)} fusion(bf16[625,2,3072]{2,1,0:T(2,128)(2,1)} %bitcast.84, s32[1024]{0:T(1024)S(1)} %get-tuple-element.328), kind=kCustom, calls=%fused_computation.clone | custom fusion | bytes 6292480 | tf_op jit(solution)/shard_map/jit(_take)/gather | solution.py:59
  51.2 16.5 %gather_fusion.1 = bf16[256,2,3072]{2,1,0:T(2,128)(2,1)} fusion(bf16[625,2,3072]{2,1,0:T(2,128)(2,1)} %bitcast.85, s32[1024]{0:T(1024)S(1)} %get-tuple-element.327), kind=kCustom, calls=%fused_computation.1.clone | custom fusion | bytes 6292480 | tf_op jit(solution)/shard_map/jit(_take)/gather | solution.py:61
  68.2 16.6 %gather_fusion.4 = bf16[256,2,3072]{2,1,0:T(2,128)(2,1)} fusion(bf16[625,2,3072]{2,1,0:T(2,128)(2,1)} %bitcast.86, s32[1024]{0:T(1024)S(1)} %pad_clamp_fusion.1), kind=kCustom, calls=%fused_computation.4.clone | custom fusion | bytes 6292480 | tf_op jit(solution)/shard_map/jit(_take)/gather | solution.py:59
  85.0 5.5 fusion.65
  90.5 5.5 fusion.63
  96.0 5.6 fusion.67
  101.6 240.8 %collective-permute-done = bf16[625,2,3072]{2,1,0:T(2,128)(2,1)} collective-permute-done((bf16[625,2,3072]{2,1,0:T(2,128)(2,1)}, bf16[625,2,3072]{2,1,0:T(2,128)(2,1)}, u32[]{:S(2)}, u32[]{:S(2)}) %collective-permute-start) | collective-permute-done | bytes 7680032 | tf_op jit(solution)/shard_map/ppermute | solution.py:25
  342.4 16.5 %gather_fusion.3 = bf16[256,2,3072]{2,1,0:T(2,128)(2,1)} fusion(bf16[625,2,3072]{2,1,0:T(2,128)(2,1)} %collective-permute-done, s32[1024]{0:T(1024)S(1)} %pad_clamp_fusion.2), kind=kCustom, calls=%fused_computation.3.clone | custom fusion | bytes 6292480 | tf_op jit(solution)/shard_map/jit(_take)/gather | solution.py:64
  358.9 7.6 fusion.66
  366.6 12.3 %add_convert_fusion.1 = (bf16[256,1,3072]{2,1,0:T(2,128)(2,1)S(1)}, bf16[256,1,3072]{2,1,0:T(2,128)(2,1)S(1)}) fusion(f32[256,2,3072]{2,1,0:T(2,128)} %fusion.66, f32[256,2,3072]{2,1,0:T(2,128)S(1)} %bitcast.80), kind=kLoop, calls=%fused_computation.85 | loop fusion | flops 6291456 | bytes 15728640 | tf_op jit(solution)/shard_map/convert.13
  381.9 118.2 %while.40 = (s32[]{:T(128)}, f32[4,512,256]{2,1,0:T(8,128)S(1)}, s32[4]{0:T(128)S(1)}, bf16[256,6144]{1,0:T(8,128)(2,1)}, s32[]{:T(128)}, /*index=5*/s32[]{:T(128)}) while((s32[]{:T(128)}, f32[4,512,256]{2,1,0:T(8,128)S(1)}, s32[4]{0:T(128)S(1)}, bf16[256,6144]{1,0:T(8,128)(2,1)}, s32[]{:T(128)}, /*index=5*/s32[]{:T(128)}) %tuple.118), condition=%wide.region_4.6_spmd.clone, body=%wide.region_3.5_spmd.clone.sunk | while | flops 1642208256 | bytes 28864632 | solution.py:86
  383.3 26.3 %cosine_convert_fusion.7 = (bf16[512,3072]{1,0:T(8,128)(2,1)S(1)}, bf16[512,3072]{1,0:T(8,128)(2,1)S(1)}) fusion(s32[3072]{0:T(1024)S(1)} %add_add_fusion.14, s32[512]{0:T(512)S(1)} %add_add_fusion.15), kind=kLoop, calls=%fused_computation.36.clone.1 | loop fusion | flops 18874368 | bytes 6305792 | tf_op jit(solution)/shard_map/convert.2
  412.8 26.3 %cosine_convert_fusion.7 = (bf16[512,3072]{1,0:T(8,128)(2,1)S(1)}, bf16[512,3072]{1,0:T(8,128)(2,1)S(1)}) fusion(s32[3072]{0:T(1024)S(1)} %add_add_fusion.14, s32[512]{0:T(512)S(1)} %add_add_fusion.15), kind=kLoop, calls=%fused_computation.36.clone.1 | loop fusion | flops 18874368 | bytes 6305792 | tf_op jit(solution)/shard_map/convert.2
  442.4 26.3 %cosine_convert_fusion.7 = (bf16[512,3072]{1,0:T(8,128)(2,1)S(1)}, bf16[512,3072]{1,0:T(8,128)(2,1)S(1)}) fusion(s32[3072]{0:T(1024)S(1)} %add_add_fusion.14, s32[512]{0:T(512)S(1)} %add_add_fusion.15), kind=kLoop, calls=%fused_computation.36.clone.1 | loop fusion | flops 18874368 | bytes 6305792 | tf_op jit(solution)/shard_map/convert.2
  471.9 26.3 %cosine_convert_fusion.7 = (bf16[512,3072]{1,0:T(8,128)(2,1)S(1)}, bf16[512,3072]{1,0:T(8,128)(2,1)S(1)}) fusion(s32[3072]{0:T(1024)S(1)} %add_add_fusion.14, s32[512]{0:T(512)S(1)} %add_add_fusion.15), kind=kLoop, calls=%fused_computation.36.clone.1 | loop fusion | flops 18874368 | bytes 6305792 | tf_op jit(solution)/shard_map/convert.2
  501.7 16.7 %gather_fusion.5 = bf16[256,2,3072]{2,1,0:T(2,128)(2,1)} fusion(bf16[625,2,3072]{2,1,0:T(2,128)(2,1)} %collective-permute-done.2, s32[1024]{0:T(1024)S(1)} %pad_clamp_fusion), kind=kCustom, calls=%fused_computation.5.clone | custom fusion | bytes 6292480 | tf_op jit(solution)/shard_map/jit(_take)/gather | solution.py:64
  518.4 7.6 fusion.68
  526.0 12.4 %add_convert_fusion = (bf16[256,1,3072]{2,1,0:T(2,128)(2,1)S(1)}, bf16[256,1,3072]{2,1,0:T(2,128)(2,1)S(1)}) fusion(f32[256,2,3072]{2,1,0:T(2,128)} %fusion.68, f32[256,2,3072]{2,1,0:T(2,128)S(1)} %bitcast.78), kind=kLoop, calls=%fused_computation.83 | loop fusion | flops 6291456 | bytes 15728640 | tf_op jit(solution)/shard_map/convert.9
  542.8 121.2 %while.41 = (s32[]{:T(128)}, f32[4,512,256]{2,1,0:T(8,128)}, s32[4]{0:T(128)S(1)}, bf16[256,6144]{1,0:T(8,128)(2,1)}, s32[]{:T(128)}, /*index=5*/s32[]{:T(128)}) while((s32[]{:T(128)}, f32[4,512,256]{2,1,0:T(8,128)}, s32[4]{0:T(128)S(1)}, bf16[256,6144]{1,0:T(8,128)(2,1)}, s32[]{:T(128)}, /*index=5*/s32[]{:T(128)}) %tuple.132), condition=%wide.region_7.9_spmd.clone, body=%wide.region_6.8_spmd.clone.sunk | while | flops 1642208256 | bytes 28865140 | solution.py:86
  544.4 26.3 %cosine_convert_fusion.8 = (bf16[512,3072]{1,0:T(8,128)(2,1)S(1)}, bf16[512,3072]{1,0:T(8,128)(2,1)S(1)}) fusion(s32[3072]{0:T(1024)S(1)} %add_add_fusion.16, s32[512]{0:T(512)S(1)} %add_add_fusion.17), kind=kLoop, calls=%fused_computation.55.clone.1 | loop fusion | flops 18874368 | bytes 6305792 | tf_op jit(solution)/shard_map/convert.4
  570.7 2.6 fusion.122
  574.6 26.3 %cosine_convert_fusion.8 = (bf16[512,3072]{1,0:T(8,128)(2,1)S(1)}, bf16[512,3072]{1,0:T(8,128)(2,1)S(1)}) fusion(s32[3072]{0:T(1024)S(1)} %add_add_fusion.16, s32[512]{0:T(512)S(1)} %add_add_fusion.17), kind=kLoop, calls=%fused_computation.55.clone.1 | loop fusion | flops 18874368 | bytes 6305792 | tf_op jit(solution)/shard_map/convert.4
  601.0 2.6 fusion.122
  604.8 26.3 %cosine_convert_fusion.8 = (bf16[512,3072]{1,0:T(8,128)(2,1)S(1)}, bf16[512,3072]{1,0:T(8,128)(2,1)S(1)}) fusion(s32[3072]{0:T(1024)S(1)} %add_add_fusion.16, s32[512]{0:T(512)S(1)} %add_add_fusion.17), kind=kLoop, calls=%fused_computation.55.clone.1 | loop fusion | flops 18874368 | bytes 6305792 | tf_op jit(solution)/shard_map/convert.4
  631.2 2.6 fusion.122
  635.0 26.3 %cosine_convert_fusion.8 = (bf16[512,3072]{1,0:T(8,128)(2,1)S(1)}, bf16[512,3072]{1,0:T(8,128)(2,1)S(1)}) fusion(s32[3072]{0:T(1024)S(1)} %add_add_fusion.16, s32[512]{0:T(512)S(1)} %add_add_fusion.17), kind=kLoop, calls=%fused_computation.55.clone.1 | loop fusion | flops 18874368 | bytes 6305792 | tf_op jit(solution)/shard_map/convert.4
  661.4 2.6 fusion.122
  664.1 2.8 fusion.64
  667.0 12.0 %add_convert_fusion.2 = (bf16[256,1,3072]{2,1,0:T(2,128)(2,1)S(1)}, bf16[256,1,3072]{2,1,0:T(2,128)(2,1)S(1)}) fusion(f32[256,2,3072]{2,1,0:T(2,128)S(1)} %fusion.64, f32[256,2,3072]{2,1,0:T(2,128)} %fusion.63), kind=kLoop, calls=%fused_computation.87 | loop fusion | flops 6291456 | bytes 15728640 | tf_op jit(solution)/shard_map/convert.17
  684.0 5.8 fusion.75
  689.8 11.1 %reduce-scatter.8.cloned.1.call-done = f32[1024,256]{1,0:T(8,128)} async-done(((f32[2048,256]{1,0:T(8,128)}), f32[1024,256]{1,0:T(8,128)}) %reduce-scatter.8.cloned.1.call-update) | async-done | bytes 1048592 | tf_op jit(solution)/shard_map/reduce_scatter | solution.py:85
  701.0 5.7 fusion.81
  706.7 2.7 collective-permute-start.3
  709.6 117.7 %while.39 = (s32[]{:T(128)}, f32[4,512,256]{2,1,0:T(8,128)S(1)}, s32[4]{0:T(128)S(1)}, bf16[256,6144]{1,0:T(8,128)(2,1)}, s32[]{:T(128)}, /*index=5*/s32[]{:T(128)}) while((s32[]{:T(128)}, f32[4,512,256]{2,1,0:T(8,128)S(1)}, s32[4]{0:T(128)S(1)}, bf16[256,6144]{1,0:T(8,128)(2,1)}, s32[]{:T(128)}, /*index=5*/s32[]{:T(128)}) %tuple.133), condition=%wide.region_1.3_spmd.clone, body=%wide.region_0.0_spmd.clone.sunk | while | flops 1642208256 | bytes 28864632 | solution.py:86
  710.9 26.3 %cosine_convert_fusion.6 = (bf16[512,3072]{1,0:T(8,128)(2,1)S(1)}, bf16[512,3072]{1,0:T(8,128)(2,1)S(1)}) fusion(s32[3072]{0:T(1024)S(1)} %add_add_fusion.12, s32[512]{0:T(512)S(1)} %add_add_fusion.13), kind=kLoop, calls=%fused_computation.17.clone.1 | loop fusion | flops 18874368 | bytes 6305792 | tf_op jit(solution)/shard_map/convert
  740.3 26.3 %cosine_convert_fusion.6 = (bf16[512,3072]{1,0:T(8,128)(2,1)S(1)}, bf16[512,3072]{1,0:T(8,128)(2,1)S(1)}) fusion(s32[3072]{0:T(1024)S(1)} %add_add_fusion.12, s32[512]{0:T(512)S(1)} %add_add_fusion.13), kind=kLoop, calls=%fused_computation.17.clone.1 | loop fusion | flops 18874368 | bytes 6305792 | tf_op jit(solution)/shard_map/convert
  769.7 26.3 %cosine_convert_fusion.6 = (bf16[512,3072]{1,0:T(8,128)(2,1)S(1)}, bf16[512,3072]{1,0:T(8,128)(2,1)S(1)}) fusion(s32[3072]{0:T(1024)S(1)} %add_add_fusion.12, s32[512]{0:T(512)S(1)} %add_add_fusion.13), kind=kLoop, calls=%fused_computation.17.clone.1 | loop fusion | flops 18874368 | bytes 6305792 | tf_op jit(solution)/shard_map/convert
  799.2 26.3 %cosine_convert_fusion.6 = (bf16[512,3072]{1,0:T(8,128)(2,1)S(1)}, bf16[512,3072]{1,0:T(8,128)(2,1)S(1)}) fusion(s32[3072]{0:T(1024)S(1)} %add_add_fusion.12, s32[512]{0:T(512)S(1)} %add_add_fusion.13), kind=kLoop, calls=%fused_computation.17.clone.1 | loop fusion | flops 18874368 | bytes 6305792 | tf_op jit(solution)/shard_map/convert
  830.8 32.4 %reduce-scatter.4.cloned.1.call-done = f32[1024,256]{1,0:T(8,128)} async-done(((f32[2048,256]{1,0:T(8,128)}), f32[1024,256]{1,0:T(8,128)}) %reduce-scatter.4.cloned.1.call-update) | async-done | bytes 1048592 | tf_op jit(solution)/shard_map/reduce_scatter | solution.py:85
  863.3 3.6 fusion.70
  866.9 2.3 fusion.78
  869.1 47.5 %collective-permute-done.3 = f32[1250,1024]{1,0:T(8,128)} collective-permute-done((f32[1250,1024]{1,0:T(8,128)}, f32[1250,1024]{1,0:T(8,128)}, u32[]{:S(2)}, u32[]{:S(2)}) %collective-permute-start.3) | collective-permute-done | bytes 5120032 | tf_op jit(solution)/shard_map/ppermute | solution.py:25
  916.6 9.4 add_bitcast_fusion
  926.0 132.1 %all-gather.4.cloned.1.call-done = f32[4,1250,1024]{2,1,0:T(8,128)} async-done(((f32[1,1250,1024]{2,1,0:T(8,128)}), f32[4,1250,1024]{2,1,0:T(8,128)}) %all-gather.4.cloned.1.call-update) | async-done | bytes 20480016 | tf_op jit(solution)/shard_map/all_gather | solution.py:16
  1058.1 10.3 reduce_sum.9
  1068.5 7.3 reshape.172
  (150 shorter events, 53.3 us)
Async XLA Ops:
  6.5 677.5 %reduce-scatter.6.cloned.1.call-start = ((), (), s32[]{:S(2)}) async-start(), calls=%async_computation.4 | async-start | bytes 3145728 | tf_op jit(solution)/shard_map/reduce_scatter | solution.py:85
  6.5 335.9 %collective-permute-start = (bf16[625,2,3072]{2,1,0:T(2,128)(2,1)}, bf16[625,2,3072]{2,1,0:T(2,128)(2,1)}, u32[]{:S(2)}, u32[]{:S(2)}) collective-permute-start(bf16[625,2,3072]{2,1,0:T(2,128)(2,1)} %bitcast.81), channel_id=1, source_target_pairs={{8,0},{16,8},{24,16},{32,24},{40,32},{48,40},{56,48},{64,56},{72,6... | collective-permute-start | bytes 23040008 | tf_op jit(solution)/shard_map/ppermute | solution.py:25
  13.6 488.1 %collective-permute-start.2 = (bf16[625,2,3072]{2,1,0:T(2,128)(2,1)}, bf16[625,2,3072]{2,1,0:T(2,128)(2,1)}, u32[]{:S(2)}, u32[]{:S(2)}) collective-permute-start(bf16[625,2,3072]{2,1,0:T(2,128)(2,1)} %bitcast.82), channel_id=1, source_target_pairs={{16,0},{24,8},{32,16},{40,24},{48,32},{56,40},{64,48},{72,56},{80,... | collective-permute-start | bytes 23040008 | tf_op jit(solution)/shard_map/ppermute | solution.py:25
  85.0 5.5 copy-start.1
  90.5 5.5 copy-start.2
  342.4 24.1 %slice-start.2 = ((s8[6291456]{0:T(1024)(128)(4,1)}), s8[2097152]{0:T(1024)(128)(4,1)S(1)}, s32[]{:S(2)}) async-start(s8[6291456]{0:T(1024)(128)(4,1)} %bitcast.79), calls=%async_computation.9 | async-start | bytes 4194304
  358.9 7.6 slice-start.3
  383.3 26.3 %copy-start.8 = (bf16[256,6144]{1,0:T(8,128)(2,1)S(1)}, bf16[256,6144]{1,0:T(8,128)(2,1)}, u32[]{:S(2)}) copy-start(bf16[256,6144]{1,0:T(8,128)(2,1)} %get-tuple-element.467) | copy-start | bytes 9437188 | tf_op jit(solution)/shard_map/while
  412.8 26.3 %copy-start.8 = (bf16[256,6144]{1,0:T(8,128)(2,1)S(1)}, bf16[256,6144]{1,0:T(8,128)(2,1)}, u32[]{:S(2)}) copy-start(bf16[256,6144]{1,0:T(8,128)(2,1)} %get-tuple-element.467) | copy-start | bytes 9437188 | tf_op jit(solution)/shard_map/while
  442.4 26.3 %copy-start.8 = (bf16[256,6144]{1,0:T(8,128)(2,1)S(1)}, bf16[256,6144]{1,0:T(8,128)(2,1)}, u32[]{:S(2)}) copy-start(bf16[256,6144]{1,0:T(8,128)(2,1)} %get-tuple-element.467) | copy-start | bytes 9437188 | tf_op jit(solution)/shard_map/while
  471.9 26.3 %copy-start.8 = (bf16[256,6144]{1,0:T(8,128)(2,1)S(1)}, bf16[256,6144]{1,0:T(8,128)(2,1)}, u32[]{:S(2)}) copy-start(bf16[256,6144]{1,0:T(8,128)(2,1)} %get-tuple-element.467) | copy-start | bytes 9437188 | tf_op jit(solution)/shard_map/while
  500.1 1.4 copy-start.3
  501.6 199.4 %reduce-scatter.8.cloned.1.call-start = ((), (), s32[]{:S(2)}) async-start(), calls=%async_computation.5 | async-start | bytes 3145728 | tf_op jit(solution)/shard_map/reduce_scatter | solution.py:85
  501.7 24.3 %slice-start = ((s8[6291456]{0:T(1024)(128)(4,1)}), s8[2097152]{0:T(1024)(128)(4,1)S(1)}, s32[]{:S(2)}) async-start(s8[6291456]{0:T(1024)(128)(4,1)} %bitcast.77), calls=%async_computation.7 | async-start | bytes 4194304
  518.4 7.6 slice-start.1
  542.8 121.3 %copy-start = (bf16[256,2,3072]{2,1,0:T(2,128)(2,1)S(1)}, bf16[256,2,3072]{2,1,0:T(2,128)(2,1)}, u32[]{:S(2)}) copy-start(bf16[256,2,3072]{2,1,0:T(2,128)(2,1)} %gather_fusion.1) | copy-start | bytes 9437188
  544.4 26.3 %copy-start.9 = (bf16[256,6144]{1,0:T(8,128)(2,1)S(1)}, bf16[256,6144]{1,0:T(8,128)(2,1)}, u32[]{:S(2)}) copy-start(bf16[256,6144]{1,0:T(8,128)(2,1)} %get-tuple-element.449) | copy-start | bytes 9437188 | tf_op jit(solution)/shard_map/while
  574.6 26.3 %copy-start.9 = (bf16[256,6144]{1,0:T(8,128)(2,1)S(1)}, bf16[256,6144]{1,0:T(8,128)(2,1)}, u32[]{:S(2)}) copy-start(bf16[256,6144]{1,0:T(8,128)(2,1)} %get-tuple-element.449) | copy-start | bytes 9437188 | tf_op jit(solution)/shard_map/while
  604.8 26.3 %copy-start.9 = (bf16[256,6144]{1,0:T(8,128)(2,1)S(1)}, bf16[256,6144]{1,0:T(8,128)(2,1)}, u32[]{:S(2)}) copy-start(bf16[256,6144]{1,0:T(8,128)(2,1)} %get-tuple-element.449) | copy-start | bytes 9437188 | tf_op jit(solution)/shard_map/while
  635.0 26.3 %copy-start.9 = (bf16[256,6144]{1,0:T(8,128)(2,1)S(1)}, bf16[256,6144]{1,0:T(8,128)(2,1)}, u32[]{:S(2)}) copy-start(bf16[256,6144]{1,0:T(8,128)(2,1)} %get-tuple-element.449) | copy-start | bytes 9437188 | tf_op jit(solution)/shard_map/while
  664.0 199.2 %reduce-scatter.4.cloned.1.call-start = ((), (), s32[]{:S(2)}) async-start(), calls=%async_computation.3 | async-start | bytes 3145728 | tf_op jit(solution)/shard_map/reduce_scatter | solution.py:85
  679.5 0.7 copy-start.15
  689.8 179.3 %collective-permute-start.1 = (f32[1250,1024]{1,0:T(8,128)}, f32[1250,1024]{1,0:T(8,128)}, u32[]{:S(2)}, u32[]{:S(2)}) collective-permute-start(f32[1250,1024]{1,0:T(8,128)} %fusion.75), channel_id=1, source_target_pairs={{120,0},{0,8},{8,16},{16,24},{24,32},{32,40},{40,48},{48,56},{56,6... | collective-permute-start | bytes 15360008 | tf_op jit(solution)/shard_map/ppermute | solution.py:25
  706.7 209.9 %collective-permute-start.3 = (f32[1250,1024]{1,0:T(8,128)}, f32[1250,1024]{1,0:T(8,128)}, u32[]{:S(2)}, u32[]{:S(2)}) collective-permute-start(f32[1250,1024]{1,0:T(8,128)} %fusion.81), channel_id=1, source_target_pairs={{112,0},{120,8},{0,16},{8,24},{16,32},{24,40},{32,48},{40,56},{48,... | collective-permute-start | bytes 15360008 | tf_op jit(solution)/shard_map/ppermute | solution.py:25
  709.6 120.0 %copy-start.13 = (pred[256]{0:T(512)(128)(4,1)S(1)}, pred[256]{0:T(512)(128)(4,1)}, u32[]{:S(2)}) copy-start(pred[256]{0:T(512)(128)(4,1)} %get-tuple-element.249) | copy-start | bytes 772
  709.6 120.0 %copy-start.14 = (pred[256]{0:T(512)(128)(4,1)S(1)}, pred[256]{0:T(512)(128)(4,1)}, u32[]{:S(2)}) copy-start(pred[256]{0:T(512)(128)(4,1)} %get-tuple-element.253) | copy-start | bytes 772
  709.6 153.6 %copy-start.11 = (s32[256]{0:T(256)S(1)}, s32[256]{0:T(256)}, u32[]{:S(2)}) copy-start(s32[256]{0:T(256)} %get-tuple-element.312) | copy-start | bytes 3076
  710.9 26.3 %copy-start.7 = (bf16[256,6144]{1,0:T(8,128)(2,1)S(1)}, bf16[256,6144]{1,0:T(8,128)(2,1)}, u32[]{:S(2)}) copy-start(bf16[256,6144]{1,0:T(8,128)(2,1)} %get-tuple-element.485) | copy-start | bytes 9437188 | tf_op jit(solution)/shard_map/while
  740.3 26.3 %copy-start.7 = (bf16[256,6144]{1,0:T(8,128)(2,1)S(1)}, bf16[256,6144]{1,0:T(8,128)(2,1)}, u32[]{:S(2)}) copy-start(bf16[256,6144]{1,0:T(8,128)(2,1)} %get-tuple-element.485) | copy-start | bytes 9437188 | tf_op jit(solution)/shard_map/while
  769.7 26.3 %copy-start.7 = (bf16[256,6144]{1,0:T(8,128)(2,1)S(1)}, bf16[256,6144]{1,0:T(8,128)(2,1)}, u32[]{:S(2)}) copy-start(bf16[256,6144]{1,0:T(8,128)(2,1)} %get-tuple-element.485) | copy-start | bytes 9437188 | tf_op jit(solution)/shard_map/while
  799.2 26.3 %copy-start.7 = (bf16[256,6144]{1,0:T(8,128)(2,1)S(1)}, bf16[256,6144]{1,0:T(8,128)(2,1)}, u32[]{:S(2)}) copy-start(bf16[256,6144]{1,0:T(8,128)(2,1)} %get-tuple-element.485) | copy-start | bytes 9437188 | tf_op jit(solution)/shard_map/while
  827.4 1.3 copy-start.4
  828.7 229.4 %all-gather.4.cloned.1.call-start = ((), (), s32[]{:S(2)}) async-start(), calls=%async_computation.6 | async-start | bytes 25722880 | tf_op jit(solution)/shard_map/all_gather | solution.py:16
  863.3 3.6 copy-start.6
  863.3 3.6 copy-start.10
  866.8 49.8 %copy-start.5 = (f32[1024,256]{1,0:T(8,128)S(1)}, f32[1024,256]{1,0:T(8,128)}, u32[]{:S(2)}) copy-start(f32[1024,256]{1,0:T(8,128)} %reduce-scatter.6.cloned.1.call-done) | copy-start | bytes 3145732
  866.9 49.7 %copy-start.12 = (s32[256]{0:T(256)S(1)}, s32[256]{0:T(256)}, u32[]{:S(2)}) copy-start(s32[256]{0:T(256)} %get-tuple-element.308) | copy-start | bytes 3076
Sparse Core Ops, SparseCore 0:
  501.7 36.7 reduce-scatter.5
  664.2 36.7 reduce-scatter.7
  828.8 34.3 reduce-scatter.3
  926.1 131.9 all-gather.3
